TPU v7x, 32 devices: a whole 2x2x4 slice. The times are simulated.
32 devices in a mesh: row: 8 (over z, y), col: 4 (over x, core).
Axes of the slice: x: 2, y: 2, z: 4, core: 2. Of those that a mesh axis runs over, the one named last changes fastest.
Arguments:
- rhs: float32 [32768, 256], P(('row', 'col')), may hold values from -8 to 8
- front_factor: float32 [32768, 1024], P(('row', 'col')), may hold values from -1 to 4, as said below
- coupling: bfloat16 [57344, 1024], P(('row', 'col')), may hold values from -0.1875 to 0.1875
- bound_count: int32 [32], P(('row', 'col')), may hold values from 448 to 1792, as said below
- sep_owner: int32 [32, 16], P(('row', 'col')), may hold values from 0 to 31, as said below
- sep_index: int32 [32, 1792], P(('row', 'col')), may hold values from 0 to 511
- sep_rhs: float32 [16384, 256], P(('row', 'col')), may hold values from -6 to 6
- sep_factor: float32 [16384, 512], P(('row', 'col')), may hold values from -1 to 4, as said below
- cell_weight: float32 [4096, 8], P(('row', 'col')), may hold values from 0.02 to 0.3
- cell_pivot: int32 [4096, 8], P(('row', 'col')), may hold values from 0 to 1023
Outputs:
- sep_potential: float32 [16384, 256], P(('row', 'col'))
- hess: float32 [4096, 4096], P('row', 'col')
Inputs may be any that keep to these rules, and one draw needn't show every extreme that they name: `front_factor`: each block of 1024 rows is lower triangular with diagonal entries 1 or more. `sep_factor`: each block of 512 rows is lower triangular with diagonal entries 1 or more. `bound_count`: some front has all 1792 boundary rows live. `sep_owner`: each row names 16 distinct separator blocks.
All inputs are finite; a program needn't handle non-finite values.
Results may differ from a plain program's by a relative error of at most 0.0031.
Values may be sent and summed in bfloat16 or wider, within the bound.
A program may use at most 128 MiB of HBM per device.

v0:
```python
import jax
import jax.numpy as jnp
from jax import lax
from jax.sharding import PartitionSpec as P


def front_solve(factor, right):
    half_way = jax.scipy.linalg.solve_triangular(factor, right, lower=True)
    return jax.scipy.linalg.solve_triangular(factor, half_way, trans=1, lower=True)


def local(
    rhs,
    front_factor,
    coupling,
    bound_count,
    sep_owner,
    sep_index,
    sep_rhs,
    sep_factor,
    cell_weight,
    cell_pivot,
):
    row_count = lax.axis_size("row")
    col_count = lax.axis_size("col")
    fronts = row_count * col_count
    bound = coupling.shape[0]
    sources = rhs.shape[1]
    sep_size = sep_rhs.shape[0]
    halves = sep_owner.shape[1]
    slots = bound // halves
    living = jnp.arange(bound, dtype=jnp.int32) < bound_count[0]
    live_float = living.astype(jnp.float32)[:, None]
    live_half = living.astype(jnp.bfloat16)[:, None]
    owners = sep_owner[0]
    solved = front_solve(front_factor, rhs).astype(jnp.bfloat16)
    contrib = (jnp.dot(coupling, solved, preferred_element_type=jnp.float32) * live_float).astype(
        jnp.bfloat16
    )
    outgoing = (
        jnp.zeros((fronts, slots, sources), jnp.bfloat16)
        .at[owners]
        .set(contrib.reshape(halves, slots, sources))
    )
    out_index = (
        jnp.zeros((fronts, slots), jnp.int32).at[owners].set(sep_index[0].reshape(halves, slots))
    )
    incoming, in_index = (
        lax.all_to_all(outgoing, ("row", "col"), split_axis=0, concat_axis=0, tiled=True),
        lax.all_to_all(out_index, ("row", "col"), split_axis=0, concat_axis=0, tiled=True),
    )
    received = incoming.reshape(fronts * slots, sources)
    flat_index = in_index.reshape(fronts * slots)
    selector = (jnp.arange(sep_size, dtype=jnp.int32)[:, None] == flat_index[None, :]).astype(
        jnp.bfloat16
    )
    totals = jnp.dot(selector, received, preferred_element_type=jnp.float32)
    sep_potential = front_solve(sep_factor, sep_rhs - totals)
    sep_half = sep_potential.astype(jnp.bfloat16)
    replies = lax.dot_general(
        selector, sep_half, (((0,), (0,)), ((), ())), preferred_element_type=jnp.float32
    ).astype(jnp.bfloat16)
    returned = lax.all_to_all(
        replies.reshape(fronts, slots, sources),
        ("row", "col"),
        split_axis=0,
        concat_axis=0,
        tiled=True,
    )
    values = returned[owners].reshape(bound, sources) * live_half
    lifted = lax.dot_general(
        coupling, values, (((0,), (0,)), ((), ())), preferred_element_type=jnp.float32
    )
    potential = front_solve(front_factor, rhs - lifted)
    picked = potential[cell_pivot]
    field = jnp.sum(cell_weight[:, :, None] * picked, axis=1).astype(jnp.bfloat16)
    scale = 1.0 / sources
    row_tile = lax.all_gather(field, "col", axis=0, tiled=True)
    gram = (
        lax.dot_general(
            row_tile,
            lax.all_gather(field, "row", axis=0, tiled=True),
            (((1,), (1,)), ((), ())),
            preferred_element_type=jnp.float32,
        )
        * scale
    )
    hess = gram * gram
    return (sep_potential, hess)


def solution(mesh):
    placed = (
        P(("row", "col"), None),
        P(("row", "col"), None),
        P(("row", "col"), None),
        P(("row", "col")),
        P(("row", "col"), None),
        P(("row", "col"), None),
        P(("row", "col"), None),
        P(("row", "col"), None),
        P(("row", "col"), None),
        P(("row", "col"), None),
    )
    return jax.shard_map(
        local,
        mesh=mesh,
        in_specs=placed,
        out_specs=(P(("row", "col"), None), P("row", "col")),
        check_vma=False,
    )
```

profile of v0, /device:TPU:0, one launch (start us, length us, event | category | flops | bytes accessed | tf_op | source)
XLA Modules:
  0.0 324.2 jit_solution(569961011782303767)
XLA Ops:
  3.3 7.3 %all-to-all-start = ((s32[32,1,112]{2,1,0:T(1,128)}), s32[32,1,112]{2,1,0:T(1,128)S(1)}, u32[]{:S(2)}, u32[]{:S(2)}) async-start(s32[32,1,112]{2,1,0:T(1,128)} %bitcast.3), calls=%async_computation | async-start | bytes 32768 | tf_op jit(solution)/shard_map/all_to_all | solution.py:50
  10.6 4.8 %fusion.3 = f32[1024,1024]{1,0:T(8,128)} fusion(f32[1024,1024]{1,0:T(8,128)} %param.15), kind=kLoop, calls=%fused_computation.13 | loop fusion | flops 2097152 | bytes 8388608 | tf_op jit(solution)/shard_map/jit(_solve_triangular)/triangular_solve | solution.py:9
  15.4 23.4 %while.10 = (s32[]{:T(128)}, f32[1024,1024]{1,0:T(8,128)}, s32[8,2]{0,1:T(2,128)S(1)}, f32[8,128,128]{2,1,0:T(8,128)S(1)}, s32[]{:T(128)}) while((s32[]{:T(128)}, f32[1024,1024]{1,0:T(8,128)}, s32[8,2]{0,1:T(2,128)S(1)}, f32[8,128,128]{2,1,0:T(8,128)S(1)}, s32[]{:T(128)}) %tuple.93), condition=%wide.while_cond.1, body=%wide.while_body.1.sunk | while | flops 2 | bytes 131181 | solution.py:9
  16.1 2.3 bitcast_dynamic-update-slice_fusion.5
  19.0 2.3 bitcast_dynamic-update-slice_fusion.5
  22.0 2.3 bitcast_dynamic-update-slice_fusion.5
  24.9 2.3 bitcast_dynamic-update-slice_fusion.5
  27.8 2.3 bitcast_dynamic-update-slice_fusion.5
  30.8 2.3 bitcast_dynamic-update-slice_fusion.5
  33.7 2.3 bitcast_dynamic-update-slice_fusion.5
  36.6 2.2 bitcast_dynamic-update-slice_fusion.5
  38.8 78.8 %custom-call.17 = f32[8,128,128]{1,2,0:T(8,128)S(1)} custom-call(f32[8,128,128]{2,1,0:T(8,128)S(1)} %get-tuple-element.41), custom_call_target="InvertDiagBlocksLowerTriangular" | custom-call | tf_op jit(solution)/shard_map/jit(_solve_triangular)/triangular_solve | solution.py:9
  136.9 3.1 scatter_fusion
  139.9 5.8 %all-to-all-start.1 = ((bf16[32,112,256]{2,1,0:T(8,128)(2,1)}), bf16[32,112,256]{2,1,0:T(8,128)(2,1)S(1)}, u32[]{:S(2)}, u32[]{:S(2)}) async-start(bf16[32,112,256]{2,1,0:T(8,128)(2,1)} %scatter_fusion), calls=%async_computation.1 | async-start | bytes 3670016 | tf_op jit(solution)/shard_map/all_to_all | solution.py:49
  147.2 10.6 %while.9 = (s32[]{:T(128)}, f32[512,512]{1,0:T(8,128)S(1)}, s32[4,2]{0,1:T(2,128)S(1)}, f32[4,128,128]{2,1,0:T(8,128)}, s32[]{:T(128)}) while((s32[]{:T(128)}, f32[512,512]{1,0:T(8,128)S(1)}, s32[4,2]{0,1:T(2,128)S(1)}, f32[4,128,128]{2,1,0:T(8,128)}, s32[]{:T(128)}) %tuple.96), condition=%wide.while_cond.2, body=%wide.while_body.2.sunk | while | flops 2 | bytes 132705 | solution.py:9
  157.7 40.8 %custom-call.13 = f32[4,128,128]{1,2,0:T(8,128)} custom-call(f32[4,128,128]{2,1,0:T(8,128)} %get-tuple-element.27), custom_call_target="InvertDiagBlocksLowerTriangular" | custom-call | tf_op jit(solution)/shard_map/jit(_solve_triangular)/triangular_solve | solution.py:9
  199.8 2.3 fusion.9
  207.5 3.3 %fusion.2 = bf16[3584,256]{1,0:T(8,128)(2,1)} fusion(s32[3584]{0:T(1024)S(1)} %eq.16, f32[512,256]{1,0:T(8,128)S(1)} %pad_maximum_fusion), kind=kOutput, calls=%fused_computation.11 | convolution fusion | flops 942407680 | bytes 2373632 | tf_op jit(solution)/shard_map/dot_general | solution.py:60
  210.8 6.2 %all-to-all-start.2 = ((bf16[32,112,256]{2,1,0:T(8,128)(2,1)}), bf16[32,112,256]{2,1,0:T(8,128)(2,1)S(1)}, u32[]{:S(2)}, u32[]{:S(2)}) async-start(bf16[32,112,256]{2,1,0:T(8,128)(2,1)} %bitcast.244), calls=%async_computation.2 | async-start | bytes 3670016 | tf_op jit(solution)/shard_map/all_to_all | solution.py:63
  218.7 41.0 %all-to-all-done.2 = bf16[32,112,256]{2,1,0:T(8,128)(2,1)S(1)} async-done(((bf16[32,112,256]{2,1,0:T(8,128)(2,1)}), bf16[32,112,256]{2,1,0:T(8,128)(2,1)S(1)}, u32[]{:S(2)}, u32[]{:S(2)}) %all-to-all-start.2) | async-done | bytes 1835040 | tf_op jit(solution)/shard_map/all_to_all | solution.py:63
  260.7 3.6 %fusion.8 = f32[1024,256]{0,1:T(8,128)S(1)} fusion(f32[1024,256]{0,1:T(8,128)} %copy.20, bf16[1792,256]{1,0:T(8,128)(2,1)S(1)} %bitcast_multiply_fusion.1, bf16[1792,1024]{1,0:T(8,128)(2,1)} %param.16), kind=kOutput, calls=%fused_computation.21 | convolution fusion | flops 939786240 | bytes 6684672 | tf_op jit(solution)/shard_map/dot_general | solution.py:71
  281.3 3.5 %gather_fusion.1 = f32[1024,256]{1,0:T(8,128)S(1)} fusion(f32[1024,256]{1,0:T(8,128)S(1)} %constant_dynamic-update-slice_fusion.79, s32[1024]{0:T(1024)S(1)} %broadcast_clamp_fusion), kind=kCustom, calls=%fused_computation.1 | custom fusion | bytes 2101248 | tf_op jit(solution)/shard_map/gather | solution.py:75
  285.1 31.3 %all_gather.7 = bf16[1024,256]{1,0:T(8,128)(2,1)S(1)} all-gather(bf16[128,256]{1,0:T(8,128)(2,1)S(1)} %fusion.10), channel_id=1, replica_groups=mesh['row'=8,'col'=4] {'row'}, dimensions={0}, use_global_device_ids=true | all-gather | bytes 589824 | tf_op jit(solution)/shard_map/all_gather | solution.py:82
  316.4 5.8 %all_gather.6 = bf16[512,256]{1,0:T(8,128)(2,1)S(1)} all-gather(bf16[128,256]{1,0:T(8,128)(2,1)S(1)} %fusion.10), channel_id=1, replica_groups=mesh['row'=8,'col'=4] {'col'}, dimensions={0}, use_global_device_ids=true | all-gather | bytes 327680 | tf_op jit(solution)/shard_map/all_gather | solution.py:78
  (197 shorter events, 65.8 us)
Async XLA Ops:
  3.3 136.7 %all-to-all-start = ((s32[32,1,112]{2,1,0:T(1,128)}), s32[32,1,112]{2,1,0:T(1,128)S(1)}, u32[]{:S(2)}, u32[]{:S(2)}) async-start(s32[32,1,112]{2,1,0:T(1,128)} %bitcast.3), calls=%async_computation | async-start | bytes 32768 | tf_op jit(solution)/shard_map/all_to_all | solution.py:50
  10.6 107.0 %copy-start.2 = (f32[1024,256]{1,0:T(8,128)S(1)}, f32[1024,256]{1,0:T(8,128)}, u32[]{:S(2)}) copy-start(f32[1024,256]{1,0:T(8,128)} %param.14) | copy-start | bytes 3145732
  117.6 5.1 %copy-start = (f32[1024,1024]{1,0:T(8,128)S(1)}, f32[1024,1024]{1,0:T(8,128)}, u32[]{:S(2)}) copy-start(f32[1024,1024]{1,0:T(8,128)} %get-tuple-element.216) | copy-start | bytes 12582916
  130.4 3.4 %copy-start.8 = (bf16[1792,1024]{1,0:T(8,128)(2,1)S(1)}, bf16[1792,1024]{1,0:T(8,128)(2,1)}, u32[]{:S(2)}) copy-start(bf16[1792,1024]{1,0:T(8,128)(2,1)} %param.16) | copy-start | bytes 11010052
  139.9 59.8 %all-to-all-start.1 = ((bf16[32,112,256]{2,1,0:T(8,128)(2,1)}), bf16[32,112,256]{2,1,0:T(8,128)(2,1)S(1)}, u32[]{:S(2)}, u32[]{:S(2)}) async-start(bf16[32,112,256]{2,1,0:T(8,128)(2,1)} %scatter_fusion), calls=%async_computation.1 | async-start | bytes 3670016 | tf_op jit(solution)/shard_map/all_to_all | solution.py:49
  199.8 2.3 copy-start.4
  206.7 0.8 copy-start.5
  207.5 9.6 %copy-start.3 = (f32[1024,256]{1,0:T(8,128)S(1)}, f32[1024,256]{1,0:T(8,128)}, u32[]{:S(2)}) copy-start(f32[1024,256]{1,0:T(8,128)} %param.14) | copy-start | bytes 3145732
  210.8 7.6 %copy-start.7 = (s32[128,8]{0,1:T(8,128)S(1)}, s32[128,8]{0,1:T(8,128)}, u32[]{:S(2)}) copy-start(s32[128,8]{0,1:T(8,128)} %param.23) | copy-start | bytes 12292
  210.8 7.8 %copy-start.6 = (f32[128,8]{0,1:T(8,128)S(1)}, f32[128,8]{0,1:T(8,128)}, u32[]{:S(2)}) copy-start(f32[128,8]{0,1:T(8,128)} %param.22) | copy-start | bytes 12292
  210.8 48.9 %all-to-all-start.2 = ((bf16[32,112,256]{2,1,0:T(8,128)(2,1)}), bf16[32,112,256]{2,1,0:T(8,128)(2,1)S(1)}, u32[]{:S(2)}, u32[]{:S(2)}) async-start(bf16[32,112,256]{2,1,0:T(8,128)(2,1)} %bitcast.244), calls=%async_computation.2 | async-start | bytes 3670016 | tf_op jit(solution)/shard_map/all_to_all | solution.py:63
  260.6 4.0 %copy-start.1 = (f32[1024,1024]{1,0:T(8,128)S(1)}, f32[1024,1024]{1,0:T(8,128)}, u32[]{:S(2)}) copy-start(f32[1024,1024]{1,0:T(8,128)} %get-tuple-element.216) | copy-start | bytes 12582916
where the time goes:
time: 328 us; the launch traced here: 324 us
  other arithmetic  128 us (39%)
  matrix products  47.8 us (15%)
  local copies, waits for them, and re-layouts  47.6 us (15%)
  waiting for transfers between devices  41 us (12%)
  blocking collectives  37.1 us (11%)
  starting transfers between devices  19.4 us (6%)
    another operation x8, other arithmetic, front_solve(): jax.scipy.linalg.solve_triangular(factor, half_way, trans=1, lower=True)  126 us
    all_to_all x1, waiting for transfers between devices, local(): lax.all_to_all(replies.reshape(fronts, slots, sources), ('row', 'col'), s...  41 us
    all_gather x1, blocking collectives, local(): lax.all_gather(field, 'row', axis=0, tiled=True)  31.3 us
    another operation x34, local copies, waits for them, and re-layouts, front_solve(): jax.scipy.linalg.solve_triangular(factor, half_way, trans=1, lower=True)  23.4 us
    another operation x37, matrix products, front_solve(): half_way = jax.scipy.linalg.solve_triangular(factor, right, lower=True)  20.1 us
    another operation x37, matrix products, front_solve(): jax.scipy.linalg.solve_triangular(factor, half_way, trans=1, lower=True)  15.5 us
    another operation x12, local copies, waits for them, and re-layouts  10.5 us
    all_to_all x1, starting transfers between devices, local(): lax.all_to_all(out_index, ('row', 'col'), split_axis=0, concat_axis=0, ti...  7.33 us
  transfers between devices with their start and end apart: 3, of which 1 were waited for; matrix products, arithmetic and copies ran while one was open for 57% of the time, Pallas kernels for 0%

commit v1 on v0

v1 whole, which is shorter than its diff:
```python
import functools

import jax
import jax.numpy as jnp
from jax import lax
from jax.experimental import pallas as pl
from jax.experimental.pallas import tpu as pltpu
from jax.sharding import PartitionSpec as P

F32 = jnp.float32
BF16 = jnp.bfloat16
NN = (((1,), (0,)), ((), ()))
NT = (((1,), (1,)), ((), ()))
VMEM_LIMIT = 63 * 1024 * 1024


def split(value):
    high = value.astype(BF16)
    return high, (value - high.astype(F32)).astype(BF16)


def dot(left, right, dims):
    return lax.dot_general(left, right, dims, preferred_element_type=F32)


def dot3(left, right, dims=NN):
    return dot(left[0], right[0], dims) + (dot(left[0], right[1], dims) + dot(left[1], right[0], dims))


def invert(factor_ref, high_ref, low_ref, work_ref):
    order = factor_ref.shape[0]
    base = work_ref.shape[1]
    count = order // base
    rows = lax.broadcasted_iota(jnp.int32, (base, base), 0)
    cols = lax.broadcasted_iota(jnp.int32, (base, base), 1)
    differ = rows ^ cols
    below = rows > cols
    high_ref[...] = jnp.zeros_like(high_ref)
    low_ref[...] = jnp.zeros_like(low_ref)

    def diagonal(block):
        return factor_ref[pl.ds(block * base, base), pl.ds(block * base, base)]

    for block in range(count):
        part = diagonal(block)
        only = jnp.where(differ == 0, part, 0.0)
        down = 1.0 / jnp.sum(only, axis=1, keepdims=True)
        across = 1.0 / jnp.sum(only, axis=0, keepdims=True)
        pairs = jnp.where(below & (differ == 1), (part * down) * across, 0.0)
        work_ref[block] = jnp.where(differ == 0, jnp.broadcast_to(down, part.shape), -pairs)
    size = 2
    while size < base:
        inside = below & (differ >= size) & (differ < 2 * size)
        for block in range(count):
            outer = split(jnp.where(inside, diagonal(block), 0.0))
            held = work_ref[block]
            parts = split(held)
            step = split(dot3(outer, parts))
            work_ref[block] = held - dot3(parts, step)
        size *= 2
    for block in range(count):
        spot = pl.ds(block * base, base)
        high, low = split(work_ref[block])
        high_ref[spot, spot] = high
        low_ref[spot, spot] = low
    size = base
    while size < order:
        for start in range(0, order, 2 * size):
            first, second = pl.ds(start, size), pl.ds(start + size, size)
            outer = split(factor_ref[second, first])
            step = split(dot3(outer, (high_ref[first, first], low_ref[first, first])))
            high, low = split(-dot3((high_ref[second, second], low_ref[second, second]), step))
            high_ref[second, first] = high
            low_ref[second, first] = low
        size *= 2


def both(parts_ref):
    return parts_ref[0][...], parts_ref[1][...]


def turned_solve(turned, high_ref, low_ref):
    inverse = (high_ref[...], low_ref[...])
    half_way = split(dot3(split(turned), inverse, NT))
    return dot3(half_way, inverse, NN)


def front_kernel(count_ref, owner_ref, factor_ref, rhs_ref, coupling_ref, out_ref, high_ref, low_ref, work_ref, contrib_ref):
    invert(factor_ref, high_ref, low_ref, work_ref)
    solved = turned_solve(rhs_ref[...].T, high_ref, low_ref).astype(BF16)
    product = dot(coupling_ref[...], solved, NT)
    rows = lax.broadcasted_iota(jnp.int32, product.shape, 0)
    contrib_ref[...] = jnp.where(rows < count_ref[0], product, 0.0).astype(BF16)
    out_ref[...] = jnp.zeros_like(out_ref)
    slots = out_ref.shape[1]
    for half in range(owner_ref.shape[1]):
        out_ref[owner_ref[0, half]] = contrib_ref[pl.ds(half * slots, slots), :]


def separator_inverse_kernel(factor_ref, high_ref, low_ref, turned_high_ref, turned_low_ref, work_ref):
    invert(factor_ref, high_ref, low_ref, work_ref)
    turned_high_ref[...] = high_ref[...].T
    turned_low_ref[...] = low_ref[...].T


def owner_kernel(row_ref, column_ref, received_ref, rhs_ref, high_ref, low_ref, turned_high_ref, turned_low_ref, out_ref, reply_ref):
    size = rhs_ref.shape[0]
    total = row_ref.shape[1]
    selector = (lax.broadcasted_iota(jnp.int32, (size, total), 0) == row_ref[...]).astype(F32).astype(BF16)
    reduced = rhs_ref[...] - dot(selector, received_ref[...], NN)
    half_way = split(dot3((high_ref[...], low_ref[...]), split(reduced)))
    potential = dot3((turned_high_ref[...], turned_low_ref[...]), half_way)
    out_ref[...] = potential
    picker = (lax.broadcasted_iota(jnp.int32, (total, size), 1) == column_ref[...]).astype(F32).astype(BF16)
    reply_ref[...] = dot(picker, potential.astype(BF16), NN).astype(BF16)


def back_kernel(count_ref, owner_ref, returned_ref, rhs_ref, coupling_ref, high_ref, low_ref, weight_ref, pivot_ref, field_ref, values_ref):
    slots = returned_ref.shape[1]
    for half in range(owner_ref.shape[1]):
        values_ref[pl.ds(half * slots, slots), :] = returned_ref[owner_ref[0, half]]
    values = values_ref[...]
    rows = lax.broadcasted_iota(jnp.int32, values.shape, 0)
    values = jnp.where(rows < count_ref[0], values.astype(F32), 0.0)
    lifted = dot(values.T.astype(BF16), coupling_ref[...], NN)
    potential = turned_solve(rhs_ref[...].T - lifted, high_ref, low_ref)
    shape = (weight_ref.shape[0], rhs_ref.shape[0])
    spots = lax.broadcasted_iota(jnp.int32, shape, 1)
    spread = jnp.zeros(shape, F32)
    for near in range(weight_ref.shape[1]):
        spread += jnp.where(spots == pivot_ref[:, near : near + 1], weight_ref[:, near : near + 1], 0.0)
    field_ref[...] = dot3(split(spread), split(potential), NT).astype(BF16)


def call(kernel, out_shape, in_specs, scratch, flops, moved, **more):
    outs = jax.tree.map(lambda _: pl.BlockSpec(memory_space=pltpu.VMEM), out_shape)
    return pl.pallas_call(
        kernel,
        out_shape=out_shape,
        in_specs=in_specs,
        out_specs=outs,
        scratch_shapes=scratch,
        cost_estimate=pl.CostEstimate(flops=flops, bytes_accessed=moved, transcendentals=0),
        compiler_params=pltpu.CompilerParams(vmem_limit_bytes=VMEM_LIMIT, **more),
    )


def local(
    rhs,
    front_factor,
    coupling,
    bound_count,
    sep_owner,
    sep_index,
    sep_rhs,
    sep_factor,
    cell_weight,
    cell_pivot,
):
    fronts = lax.axis_size("row") * lax.axis_size("col")
    bound = coupling.shape[0]
    pivots, sources = rhs.shape
    sep_size = sep_rhs.shape[0]
    halves = sep_owner.shape[1]
    slots = bound // halves
    shape = jax.ShapeDtypeStruct
    smem = pl.BlockSpec(memory_space=pltpu.SMEM)
    vmem = pl.BlockSpec(memory_space=pltpu.VMEM)
    base = 256
    owners = sep_owner[0]
    out_index = (
        jnp.full((fronts, slots), -1, jnp.int32).at[owners].set(sep_index[0].reshape(halves, slots))
    )
    in_index = lax.all_to_all(out_index, ("row", "col"), split_axis=0, concat_axis=0, tiled=True)
    outgoing, high, low = call(
        front_kernel,
        (
            shape((fronts, slots, sources), BF16),
            shape((pivots, pivots), BF16),
            shape((pivots, pivots), BF16),
        ),
        [smem, smem, vmem, vmem, vmem],
        [pltpu.VMEM((pivots // base, base, base), F32), pltpu.VMEM((bound, sources), BF16)],
        10**10,
        10**7,
    )(bound_count, sep_owner, front_factor, rhs, coupling)
    incoming = lax.all_to_all(outgoing, ("row", "col"), split_axis=0, concat_axis=0, tiled=True)
    received = incoming.reshape(fronts * slots, sources)
    inverse = call(
        separator_inverse_kernel,
        tuple(shape((sep_size, sep_size), BF16) for _ in range(4)),
        [vmem],
        [pltpu.VMEM((sep_size // base, base, base), F32)],
        10**10,
        10**7,
    )(sep_factor)
    sep_potential, replies = call(
        owner_kernel,
        (shape((sep_size, sources), F32), shape((fronts * slots, sources), BF16)),
        [vmem] * 8,
        [],
        10**9,
        10**7,
    )(in_index.reshape(1, fronts * slots), in_index.reshape(fronts * slots, 1), received, sep_rhs, *inverse)
    returned = lax.all_to_all(
        replies.reshape(fronts, slots, sources),
        ("row", "col"),
        split_axis=0,
        concat_axis=0,
        tiled=True,
    )
    field = call(
        back_kernel,
        shape((cell_weight.shape[0], sources), BF16),
        [smem, smem] + [vmem] * 7,
        [pltpu.VMEM((bound, sources), BF16)],
        10**9,
        10**7,
    )(bound_count, sep_owner, returned, rhs, coupling, high, low, cell_weight, cell_pivot)
    scale = 1.0 / sources
    row_tile = lax.all_gather(field, "col", axis=0, tiled=True)
    gram = (
        lax.dot_general(
            row_tile,
            lax.all_gather(field, "row", axis=0, tiled=True),
            NT,
            preferred_element_type=jnp.float32,
        )
        * scale
    )
    return (sep_potential, gram * gram)


def solution(mesh):
    both_axes = P(("row", "col"), None)
    placed = (both_axes, both_axes, both_axes, P(("row", "col"))) + (both_axes,) * 6
    return jax.shard_map(
        local,
        mesh=mesh,
        in_specs=placed,
        out_specs=(both_axes, P("row", "col")),
        check_vma=False,
    )
```

time: 328 us -> 186 us (0.57)
  other arithmetic: 128 us -> 2.06 us
  Pallas kernels: 0 us -> 46.3 us
  matrix products: 47.8 us -> 1.79 us
  local copies, waits for them, and re-layouts: 47.6 us -> 5.98 us
  waiting for transfers between devices: 41 us -> 72.8 us
    another operation x8 -> x0, other arithmetic: 126 us -> none  [front_solve(): jax.scipy.linalg.solve_triangular(factor, half_way, trans=1, lower=True)]
    pallas_call x0 -> x4, Pallas kernels: none -> 46.3 us  [the longest x1 18.9 us: local(): call(front_kernel, (shape((fronts, slots, sources), BF16), shape((pivots,...]
    another operation x74 -> x0, matrix products: 35.6 us -> none  [the longest x37 20.1 us: front_solve(): half_way = jax.scipy.linalg.solve_triangular(factor, right, lower=True)]
    another operation x46 -> x0, local copies, waits for them, and re-layouts: 33.9 us -> none  [the longest x34 23.4 us: front_solve(): jax.scipy.linalg.solve_triangular(factor, half_way, trans=1, lower=True)]
    all_to_all x1, waiting for transfers between devices: 0.01 us -> 31.2 us  [local(): lax.all_to_all(outgoing, ('row', 'col'), split_axis=0, concat_axis=0, til...]
    dot_general x4 -> x0, matrix products: 10.4 us -> none  [the longest x1 3.62 us: local(): lax.dot_general(coupling, values, (((0,), (0,)), ((), ())), preferred_ele...]
    gather x2 -> x0, local copies, waits for them, and re-layouts: 4.07 us -> none  [the longest x1 3.47 us: local(): picked = potential[cell_pivot]]
  transfers between devices with their start and end apart: 3 -> 3, of which waited for: 1 -> 2; matrix products, arithmetic and copies ran while one was open for 57% -> 3% of each run, Pallas kernels for 0% -> 15%
where the time goes in v1:
time: 186 us; the launch traced here: 185 us
  waiting for transfers between devices  72.8 us (39%)
  Pallas kernels  46.3 us (25%)
  blocking collectives  37.4 us (20%)
  starting transfers between devices  17.7 us (10%)
  local copies, waits for them, and re-layouts  5.98 us (3%)
  other arithmetic  2.06 us (1%)
    all_to_all x1, waiting for transfers between devices, local(): lax.all_to_all(replies.reshape(fronts, slots, sources), ('row', 'col'), s...  41.6 us
    all_gather x1, blocking collectives, local(): lax.all_gather(field, 'row', axis=0, tiled=True)  31.5 us
    all_to_all x1, waiting for transfers between devices, local(): lax.all_to_all(outgoing, ('row', 'col'), split_axis=0, concat_axis=0, til...  31.2 us
    pallas_call x1, Pallas kernels, local(): call(front_kernel, (shape((fronts, slots, sources), BF16), shape((pivots,...  18.9 us
    pallas_call x1, Pallas kernels, local(): call(back_kernel, shape((cell_weight.shape[0], sources), BF16), [smem, sm...  10.5 us
    pallas_call x1, Pallas kernels, local(): call(owner_kernel, (shape((sep_size, sources), F32), shape((fronts * slot...  8.93 us
    pallas_call x1, Pallas kernels, local(): call(separator_inverse_kernel, tuple((shape((sep_size, sep_size), BF16) f...  7.95 us
    all_to_all x1, starting transfers between devices, local(): lax.all_to_all(out_index, ('row', 'col'), split_axis=0, concat_axis=0, ti...  7.33 us
  transfers between devices with their start and end apart: 3, of which 2 were waited for; matrix products, arithmetic and copies ran while one was open for 3% of the time, Pallas kernels for 15%

profile of v1, /device:TPU:0, one launch (start us, length us, event | category | flops | bytes accessed | tf_op | source)
XLA Modules:
  0.0 185.4 jit_solution(17737902693197704387)
XLA Ops:
  0.6 0.7 reduce
  1.3 0.1 reshape.56
  1.4 0.7 fusion.2
  2.1 1.2 scatter_custom_fusion
  3.3 7.3 %all-to-all-start = ((s32[32,1,112]{2,1,0:T(1,128)}), s32[32,1,112]{2,1,0:T(1,128)S(1)}, u32[]{:S(2)}, u32[]{:S(2)}) async-start(s32[32,1,112]{2,1,0:T(1,128)} %bitcast.2), calls=%async_computation | async-start | bytes 32768 | tf_op jit(solution)/shard_map/all_to_all | solution.py:174
  11.3 18.9 %shard_map.113 = (bf16[32,112,256]{2,1,0:T(8,128)(2,1)}, bf16[1024,1024]{1,0:T(8,128)(2,1)}, bf16[1024,1024]{1,0:T(8,128)(2,1)}) custom-call(s32[1]{0:T(128)S(6)} %copy.20.count_ref, s32[1,16]{1,0:T(1,128)} %owner_ref.3, f32[1024,1024]{1,0:T(8,128)} %factor_ref.2, f32[1024,256]{1,0:T(8,128)} %rhs_ref.5, bf16[1792,1024]{1,0:T(8,128)(2,1)} %coupling_ref.3), custom_call_target="tpu_custom_call" | custom-call | flops 10000000000 | bytes 10000000 | tf_op jit(solution)/shard_map/pallas_call | solution.py:175
  30.2 0.0 all-to-all-done
  30.2 5.9 %all-to-all-start.1 = ((bf16[32,112,256]{2,1,0:T(8,128)(2,1)}), bf16[32,112,256]{2,1,0:T(8,128)(2,1)}, u32[]{:S(2)}, u32[]{:S(2)}) async-start(bf16[32,112,256]{2,1,0:T(8,128)(2,1)} %get-tuple-element.11), calls=%async_computation.1 | async-start | bytes 3670016 | tf_op jit(solution)/shard_map/all_to_all | solution.py:187
  36.2 8.0 %shard_map.114 = (bf16[512,512]{1,0:T(8,128)(2,1)}, bf16[512,512]{1,0:T(8,128)(2,1)}, bf16[512,512]{1,0:T(8,128)(2,1)}, bf16[512,512]{1,0:T(8,128)(2,1)}) custom-call(f32[512,512]{1,0:T(8,128)} %factor_ref.3), custom_call_target="tpu_custom_call" | custom-call | flops 10000000000 | bytes 10000000 | tf_op jit(solution)/shard_map/pallas_call | solution.py:189
  44.1 2.1 %reshape.60.column_ref = s32[3584,1]{1,0:T(8,128)} reshape(s32[32,112]{1,0:T(8,128)S(1)} %bitcast.11) | data formatting | bytes 28672 | tf_op jit(solution)/shard_map/reshape | solution.py:204
  46.2 0.5 broadcast.30
  46.7 0.7 reduce.6
  47.4 0.7 reshape.48.row_ref
  48.1 31.2 %all-to-all-done.1 = bf16[32,112,256]{2,1,0:T(8,128)(2,1)} async-done(((bf16[32,112,256]{2,1,0:T(8,128)(2,1)}), bf16[32,112,256]{2,1,0:T(8,128)(2,1)}, u32[]{:S(2)}, u32[]{:S(2)}) %all-to-all-start.1) | async-done | bytes 1835040 | tf_op jit(solution)/shard_map/all_to_all | solution.py:187
  79.2 8.9 %shard_map.115 = (f32[512,256]{1,0:T(8,128)}, bf16[3584,256]{1,0:T(8,128)(2,1)}) custom-call(s32[1,3584]{1,0:T(1,128)} %reshape.48.row_ref, s32[3584,1]{1,0:T(8,128)} %reshape.60.column_ref, bf16[3584,256]{1,0:T(8,128)(2,1)} %bitcast.3.received_ref, f32[512,256]{1,0:T(8,128)} %rhs_ref.4, bf16[512,512]{1,0:T(8,128)(2,1)} %get-tuple-element.12.high_ref, ...), custom_call_target="tpu_custom_call" | custom-call | flops 1000000000 | bytes 10000000 | tf_op jit(solution)/shard_map/pallas_call | solution.py:197
  88.2 4.5 %all-to-all-start.2 = ((bf16[32,112,256]{2,1,0:T(8,128)(2,1)}), bf16[32,112,256]{2,1,0:T(8,128)(2,1)}, u32[]{:S(2)}, u32[]{:S(2)}) async-start(bf16[32,112,256]{2,1,0:T(8,128)(2,1)} %bitcast.10), calls=%async_computation.2 | async-start | bytes 3670016 | tf_op jit(solution)/shard_map/all_to_all | solution.py:205
  92.6 0.0 copy-done
  92.6 0.7 copy.18.weight_ref
  93.4 0.7 copy.19.pivot_ref
  94.1 41.6 %all-to-all-done.2.returned_ref = bf16[32,112,256]{2,1,0:T(8,128)(2,1)} async-done(((bf16[32,112,256]{2,1,0:T(8,128)(2,1)}), bf16[32,112,256]{2,1,0:T(8,128)(2,1)}, u32[]{:S(2)}, u32[]{:S(2)}) %all-to-all-start.2) | async-done | bytes 1835040 | tf_op jit(solution)/shard_map/all_to_all | solution.py:205
  135.7 10.5 %shard_map.116 = bf16[128,256]{1,0:T(8,128)(2,1)} custom-call(s32[1]{0:T(128)S(6)} %copy.20.count_ref, s32[1,16]{1,0:T(1,128)} %owner_ref.3, bf16[32,112,256]{2,1,0:T(8,128)(2,1)} %all-to-all-done.2.returned_ref, f32[1024,256]{1,0:T(8,128)} %rhs_ref.5, bf16[1792,1024]{1,0:T(8,128)(2,1)} %coupling_ref.3, bf16[1024,1024]{1,0:T(8,128)(2,1)} %get-tuple-element.18.high_ref, ...), custom_call_target="tpu_custom_call" | custom-call | flops 1000000000 | bytes 10000000 | tf_op jit(solution)/shard_map/pallas_call | solution.py:212
  146.2 31.5 %all_gather.7 = bf16[1024,256]{1,0:T(8,128)(2,1)S(1)} all-gather(bf16[128,256]{1,0:T(8,128)(2,1)} %shard_map.116), channel_id=1, replica_groups=mesh['row'=8,'col'=4] {'row'}, dimensions={0}, use_global_device_ids=true | all-gather | bytes 589824 | tf_op jit(solution)/shard_map/all_gather | solution.py:225
  177.7 6.0 %all_gather.6 = bf16[512,256]{1,0:T(8,128)(2,1)S(1)} all-gather(bf16[128,256]{1,0:T(8,128)(2,1)} %shard_map.116), channel_id=1, replica_groups=mesh['row'=8,'col'=4] {'col'}, dimensions={0}, use_global_device_ids=true | all-gather | bytes 327680 | tf_op jit(solution)/shard_map/all_gather | solution.py:221
  183.6 1.8 multiply_multiply_fusion
  (3 shorter events, 0.0 us)
Async XLA Ops:
  3.3 26.9 %all-to-all-start = ((s32[32,1,112]{2,1,0:T(1,128)}), s32[32,1,112]{2,1,0:T(1,128)S(1)}, u32[]{:S(2)}, u32[]{:S(2)}) async-start(s32[32,1,112]{2,1,0:T(1,128)} %bitcast.2), calls=%async_computation | async-start | bytes 32768 | tf_op jit(solution)/shard_map/all_to_all | solution.py:174
  30.2 49.0 %all-to-all-start.1 = ((bf16[32,112,256]{2,1,0:T(8,128)(2,1)}), bf16[32,112,256]{2,1,0:T(8,128)(2,1)}, u32[]{:S(2)}, u32[]{:S(2)}) async-start(bf16[32,112,256]{2,1,0:T(8,128)(2,1)} %get-tuple-element.11), calls=%async_computation.1 | async-start | bytes 3670016 | tf_op jit(solution)/shard_map/all_to_all | solution.py:187
  88.2 4.5 %copy-start = (f32[128,8]{0,1:T(8,128)S(1)}, f32[128,8]{0,1:T(8,128)}, u32[]{:S(2)}) copy-start(f32[128,8]{0,1:T(8,128)} %param.18) | copy-start | bytes 12292
  88.2 5.2 %copy-start.1 = (s32[128,8]{0,1:T(8,128)S(1)}, s32[128,8]{0,1:T(8,128)}, u32[]{:S(2)}) copy-start(s32[128,8]{0,1:T(8,128)} %param.19) | copy-start | bytes 12292
  88.2 47.5 %all-to-all-start.2 = ((bf16[32,112,256]{2,1,0:T(8,128)(2,1)}), bf16[32,112,256]{2,1,0:T(8,128)(2,1)}, u32[]{:S(2)}, u32[]{:S(2)}) async-start(bf16[32,112,256]{2,1,0:T(8,128)(2,1)} %bitcast.10), calls=%async_computation.2 | async-start | bytes 3670016 | tf_op jit(solution)/shard_map/all_to_all | solution.py:205

commit v2 on v1

v2 whole, which is shorter than its diff:
```python
import functools

import jax
import jax.numpy as jnp
from jax import lax
from jax.experimental import pallas as pl
from jax.experimental.pallas import tpu as pltpu
from jax.sharding import PartitionSpec as P

F32 = jnp.float32
BF16 = jnp.bfloat16
NN = (((1,), (0,)), ((), ()))
NT = (((1,), (1,)), ((), ()))
VMEM_LIMIT = 63 * 1024 * 1024


def split(value):
    high = value.astype(BF16)
    return high, (value - high.astype(F32)).astype(BF16)


def dot(left, right, dims):
    return lax.dot_general(left, right, dims, preferred_element_type=F32)


def dot3(left, right, dims=NN):
    return dot(left[0], right[0], dims) + (dot(left[0], right[1], dims) + dot(left[1], right[0], dims))


def invert(factor_ref, high_ref, low_ref, work_ref):
    order = factor_ref.shape[0]
    base = work_ref.shape[1]
    count = order // base
    rows = lax.broadcasted_iota(jnp.int32, (base, base), 0)
    cols = lax.broadcasted_iota(jnp.int32, (base, base), 1)
    differ = rows ^ cols
    below = rows > cols
    high_ref[...] = jnp.zeros_like(high_ref)
    low_ref[...] = jnp.zeros_like(low_ref)

    def diagonal(block):
        return factor_ref[pl.ds(block * base, base), pl.ds(block * base, base)]

    for block in range(count):
        part = diagonal(block)
        only = jnp.where(differ == 0, part, 0.0)
        down = 1.0 / jnp.sum(only, axis=1, keepdims=True)
        across = 1.0 / jnp.sum(only, axis=0, keepdims=True)
        pairs = jnp.where(below & (differ == 1), (part * down) * across, 0.0)
        work_ref[block] = jnp.where(differ == 0, jnp.broadcast_to(down, part.shape), -pairs)
    size = 2
    while size < base:
        inside = below & (differ >= size) & (differ < 2 * size)
        for block in range(count):
            outer = split(jnp.where(inside, diagonal(block), 0.0))
            held = work_ref[block]
            parts = split(held)
            step = split(dot3(outer, parts))
            work_ref[block] = held - dot3(parts, step)
        size *= 2
    for block in range(count):
        spot = pl.ds(block * base, base)
        high, low = split(work_ref[block])
        high_ref[spot, spot] = high
        low_ref[spot, spot] = low
    size = base
    while size < order:
        for start in range(0, order, 2 * size):
            first, second = pl.ds(start, size), pl.ds(start + size, size)
            outer = split(factor_ref[second, first])
            step = split(dot3(outer, (high_ref[first, first], low_ref[first, first])))
            high, low = split(-dot3((high_ref[second, second], low_ref[second, second]), step))
            high_ref[second, first] = high
            low_ref[second, first] = low
        size *= 2


def turned_solve(turned, high_ref, low_ref):
    inverse = (high_ref[...], low_ref[...])
    half_way = split(dot3(split(turned), inverse, NT))
    return dot3(half_way, inverse, NN)


MESH = pl.DeviceIdType.MESH


def whole_kernel(
    depth,
    count_ref,
    owner_ref,
    place_ref,
    table_ref,
    factor_ref,
    rhs_ref,
    coupling_ref,
    sep_rhs_ref,
    sep_factor_ref,
    weight_ref,
    pivot_ref,
    sep_out_ref,
    row_out_ref,
    col_out_ref,
    high_ref,
    low_ref,
    work_ref,
    sep_high_ref,
    sep_low_ref,
    sep_work_ref,
    flat_ref,
    contrib_ref,
    index_out_ref,
    index_ref,
    column_ref,
    stage_ref,
    received_ref,
    chain_out_ref,
    up_ref,
    down_ref,
    own_ref,
    halves_ref,
    reply_ref,
    returned_ref,
    index_send,
    index_recv,
    out_send,
    out_recv,
    chain_send,
    up_recv,
    down_recv,
    relay_up_send,
    relay_down_send,
    relay_recv,
    reply_send,
    reply_recv,
    field_send,
    field_recv,
    next_send,
    row_send,
    row_recv,
):
    rows, cols = col_out_ref.shape[0], row_out_ref.shape[0]
    width = rows // depth
    plane = width * cols
    row, col = lax.axis_index("row"), lax.axis_index("col")
    z, y = row // width, row % width
    me = y * cols + col
    halves, slots = owner_ref.shape[1], table_ref.shape[2]
    sep_size = sep_rhs_ref.shape[0]

    def peer(spot):
        return (z * width + spot // cols, spot % cols)

    def level(spot):
        return (spot * width + y, col)

    barrier = pltpu.get_barrier_semaphore()
    for step in range(1, plane):
        pl.semaphore_signal(barrier, inc=1, device_id=peer((me + step) % plane), device_id_type=MESH)
    for step in range(1, depth):
        pl.semaphore_signal(barrier, inc=1, device_id=level((z + step) % depth), device_id_type=MESH)

    def remote(source, target, send, recv, device):
        return pltpu.make_async_remote_copy(
            src_ref=source, dst_ref=target, send_sem=send, recv_sem=recv, device_id=device, device_id_type=MESH
        )

    def index_copy(spot):
        return remote(index_out_ref.at[spot], index_ref.at[me], index_send.at[spot], index_recv.at[me], peer(spot))

    def index_arrival(spot):
        return remote(index_out_ref.at[spot], index_ref.at[spot], index_send.at[spot], index_recv.at[spot], peer(spot))

    def out_copy(high, spot):
        return remote(
            stage_ref.at[high, spot], received_ref.at[high, me], out_send.at[high, spot], out_recv.at[high, me], peer(spot)
        )

    def out_arrival(high, spot):
        return remote(
            stage_ref.at[high, spot], received_ref.at[high, spot], out_send.at[high, spot], out_recv.at[high, spot], peer(spot)
        )

    def up_copy(high):
        return remote(chain_out_ref.at[high], up_ref.at[high], chain_send.at[high], up_recv.at[high], level(z + 1))

    def down_copy(high):
        return remote(chain_out_ref.at[high], down_ref.at[high], chain_send.at[high], down_recv.at[high], level(z - 1))

    def relay_up(high):
        return remote(halves_ref.at[high], halves_ref.at[high], relay_up_send.at[high], relay_recv.at[high], level(z + 1))

    def relay_down(high):
        return remote(halves_ref.at[high], halves_ref.at[high], relay_down_send.at[high], relay_recv.at[high], level(z - 1))

    def reply_copy(high, spot):
        return remote(
            reply_ref.at[high, spot], returned_ref.at[high * plane + me], reply_send.at[high, spot], reply_recv.at[high, me], peer(spot)
        )

    def reply_arrival(high, spot):
        return remote(
            reply_ref.at[high, spot], returned_ref.at[high * plane + spot], reply_send.at[high, spot], reply_recv.at[high, spot], peer(spot)
        )

    def others(action):
        def step(offset, carry):
            action((me + offset) % plane)
            return carry

        lax.fori_loop(1, plane, step, 0)

    def levels(order, action):
        def step(at, carry):
            spot = order(at)

            @pl.when((spot >= 0) & (spot < depth))
            def _():
                action(spot)

            return carry

        lax.fori_loop(0, 2 * depth - 1, step, 0)

    def far_first(at):
        distance = depth - 1 - at // 2
        return z + distance * (1 - 2 * (at % 2))

    def near_first(at):
        return z + ((at + 1) // 2) * (1 - 2 * (at % 2))

    invert(factor_ref, high_ref, low_ref, work_ref)
    pl.semaphore_wait(barrier, plane + depth - 2)

    def fill_index(spot, carry):
        for high in range(depth):
            index_out_ref[spot, high] = table_ref[place_ref[high * plane + spot]]
        return carry

    lax.fori_loop(0, plane, fill_index, 0)
    others(lambda spot: index_copy(spot).start())
    index_ref[me] = index_out_ref[me]

    turned_rhs = rhs_ref[...].T
    solved = turned_solve(turned_rhs, high_ref, low_ref).astype(BF16)
    product = dot(coupling_ref[...], solved, NT)
    live = lax.broadcasted_iota(jnp.int32, product.shape, 0) < count_ref[0]
    flat_ref[...] = jnp.where(live, product, 0.0).astype(BF16)
    for half in range(halves):
        contrib_ref[half] = flat_ref[pl.ds(half * slots, slots), :]
    contrib_ref[halves] = jnp.zeros(contrib_ref.shape[1:], BF16)

    def send_out(high):
        def one(spot):
            stage_ref[high, spot] = contrib_ref[place_ref[high * plane + spot]]
            out_copy(high, spot).start()

        others(one)
        received_ref[high, me] = contrib_ref[place_ref[high * plane + me]]

    levels(far_first, send_out)
    invert(sep_factor_ref, sep_high_ref, sep_low_ref, sep_work_ref)
    others(lambda spot: index_arrival(spot).wait_recv())
    for high in range(depth):
        column_ref[high] = jnp.concatenate([index_ref[spot, high] for spot in range(plane)], axis=0).T

    def gather_in(high):
        others(lambda spot: out_arrival(high, spot).wait_recv())
        numbers = lax.broadcasted_iota(jnp.int32, (sep_size, slots), 0)
        own_ref[...] = jnp.zeros_like(own_ref)
        for spot in range(plane):
            selector = jnp.where(numbers == index_ref[spot, high], 1.0, 0.0).astype(BF16)
            own_ref[...] += dot(selector, received_ref[high, spot], NN)

        @pl.when((high >= z) & (z > 0))
        def _():
            remote(chain_out_ref.at[high], up_ref.at[high], chain_send.at[high], up_recv.at[high], level(z - 1)).wait_recv()
            own_ref[...] += up_ref[high].astype(F32)

        @pl.when((high <= z) & (z < depth - 1))
        def _():
            remote(chain_out_ref.at[high], down_ref.at[high], chain_send.at[high], down_recv.at[high], level(z + 1)).wait_recv()
            own_ref[...] += down_ref[high].astype(F32)

        @pl.when(high != z)
        def _():
            chain_out_ref[high] = own_ref[...].astype(BF16)

        @pl.when(high > z)
        def _():
            up_copy(high).start()

        @pl.when(high < z)
        def _():
            down_copy(high).start()

    levels(far_first, gather_in)
    reduced = (sep_rhs_ref[...] - own_ref[...]).T
    potential = turned_solve(reduced, sep_high_ref, sep_low_ref).T
    sep_out_ref[...] = potential
    halves_ref[z] = potential.astype(BF16)

    def pass_on(high):
        @pl.when(high != z)
        def _():
            remote(halves_ref.at[high], halves_ref.at[high], relay_up_send.at[high], relay_recv.at[high], level((z + 1) % depth)).wait_recv()

        @pl.when((high <= z) & (z < depth - 1))
        def _():
            relay_up(high).start()

        @pl.when((high >= z) & (z > 0))
        def _():
            relay_down(high).start()

        numbers = lax.broadcasted_iota(jnp.int32, (slots, sep_size), 1)
        for spot in range(plane):
            picker = jnp.where(numbers == column_ref[high, :, spot : spot + 1], 1.0, 0.0).astype(BF16)
            reply_ref[high, spot] = dot(picker, halves_ref[high], NN).astype(BF16)

            @pl.when(me != spot)
            def _():
                reply_copy(high, spot).start()

        returned_ref[high * plane + me] = reply_ref[high, me]

    levels(near_first, pass_on)
    shape = (weight_ref.shape[0], rhs_ref.shape[0])
    spots = lax.broadcasted_iota(jnp.int32, shape, 1)
    spread = jnp.zeros(shape, F32)
    for near in range(weight_ref.shape[1]):
        spread += jnp.where(spots == pivot_ref[:, near : near + 1], weight_ref[:, near : near + 1], 0.0)
    levels(near_first, lambda high: others(lambda spot: reply_arrival(high, spot).wait_recv()))
    for half in range(halves):
        flat_ref[pl.ds(half * slots, slots), :] = returned_ref[owner_ref[0, half]]
    values = flat_ref[...]
    live = lax.broadcasted_iota(jnp.int32, values.shape, 0) < count_ref[0]
    values = jnp.where(live, values.astype(F32), 0.0)
    lifted = dot(values.T.astype(BF16), coupling_ref[...], NN)
    potential = turned_solve(rhs_ref[...].T - lifted, high_ref, low_ref)
    field = dot3(split(spread), split(potential), NT).astype(BF16)
    col_out_ref[row] = field
    row_out_ref[col] = field

    def field_copy(step):
        return remote(
            col_out_ref.at[row], col_out_ref.at[row], field_send.at[step], field_recv.at[row], level((z + step) % depth)
        )

    def next_copy(step, turn, high):
        spot = high * width + y
        target = (z * width + (y + turn) % width, col)
        return remote(col_out_ref.at[spot], col_out_ref.at[spot], next_send.at[step, turn], field_recv.at[spot], target)

    def row_copy(step):
        return remote(
            row_out_ref.at[col], row_out_ref.at[col], row_send.at[step], row_recv.at[col], (row, (col + step) % cols)
        )

    def field_arrival(spot):
        return remote(col_out_ref.at[spot], col_out_ref.at[spot], field_send.at[0], field_recv.at[spot], level((z + 1) % depth))

    for step in range(1, depth):
        field_copy(step).start()
    for turn in range(1, width):
        next_copy(0, turn, z).start()
    for step in range(1, cols):
        row_copy(step).start()
    for step in range(1, depth):
        high = (z - step + depth) % depth
        field_arrival(high * width + y).wait_recv()
        for turn in range(1, width):
            next_copy(step, turn, high).start()
    for step in range(depth):
        high = (z - step + depth) % depth
        for turn in range(1, width):
            field_arrival(high * width + (y + turn) % width).wait_recv()
    for step in range(1, cols):
        other = (col - step + cols) % cols
        remote(row_out_ref.at[other], row_out_ref.at[other], row_send.at[step], row_recv.at[other], (row, other)).wait_recv()
    for step in range(1, cols):
        row_copy(step).wait_send()
    for step in range(1, depth):
        field_copy(step).wait_send()
    for step in range(depth):
        for turn in range(1, width):
            next_copy(step, turn, (z - step + depth) % depth).wait_send()
    others(lambda spot: index_copy(spot).wait_send())

    def finish(high):
        others(lambda spot: out_copy(high, spot).wait_send())
        others(lambda spot: reply_copy(high, spot).wait_send())

        @pl.when(high != z)
        def _():
            remote(chain_out_ref.at[high], up_ref.at[high], chain_send.at[high], up_recv.at[high], level((z + 1) % depth)).wait_send()

        @pl.when((high <= z) & (z < depth - 1))
        def _():
            relay_up(high).wait_send()

        @pl.when((high >= z) & (z > 0))
        def _():
            relay_down(high).wait_send()

    levels(near_first, finish)


def local(
    rhs,
    front_factor,
    coupling,
    bound_count,
    sep_owner,
    sep_index,
    sep_rhs,
    sep_factor,
    cell_weight,
    cell_pivot,
):
    rows, cols = lax.axis_size("row"), lax.axis_size("col")
    fronts = rows * cols
    width = max(cols // 2, 1)
    depth = rows // width
    plane = width * cols
    bound = coupling.shape[0]
    pivots, sources = rhs.shape
    sep_size = sep_rhs.shape[0]
    cells = cell_weight.shape[0]
    halves = sep_owner.shape[1]
    slots = bound // halves
    base = 256
    shape = jax.ShapeDtypeStruct
    smem = pl.BlockSpec(memory_space=pltpu.SMEM)
    vmem = pl.BlockSpec(memory_space=pltpu.VMEM)
    found = sep_owner[0][None, :] == jnp.arange(fronts, dtype=jnp.int32)[:, None]
    place = jnp.min(jnp.where(found, jnp.arange(halves, dtype=jnp.int32)[None, :], halves), axis=1)
    table = jnp.pad(sep_index.reshape(halves, 1, slots), ((0, 1), (0, 0), (0, 0)), constant_values=-1)
    dma = pltpu.SemaphoreType.DMA
    block = (sep_size, sources)
    group = (slots, sources)
    sep_potential, row_tile, col_tile = pl.pallas_call(
        functools.partial(whole_kernel, depth),
        out_shape=(
            shape(block, F32),
            shape((cols, cells, sources), BF16),
            shape((rows, cells, sources), BF16),
        ),
        in_specs=[smem] * 3 + [vmem] * 8,
        out_specs=(vmem, vmem, vmem),
        scratch_shapes=[
            pltpu.VMEM((pivots, pivots), BF16),
            pltpu.VMEM((pivots, pivots), BF16),
            pltpu.VMEM((pivots // base, base, base), F32),
            pltpu.VMEM((sep_size, sep_size), BF16),
            pltpu.VMEM((sep_size, sep_size), BF16),
            pltpu.VMEM((sep_size // base, base, base), F32),
            pltpu.VMEM((bound, sources), BF16),
            pltpu.VMEM((halves + 1,) + group, BF16),
            pltpu.VMEM((plane, depth, 1, slots), jnp.int32),
            pltpu.VMEM((plane, depth, 1, slots), jnp.int32),
            pltpu.VMEM((depth, slots, plane), jnp.int32),
            pltpu.VMEM((depth, plane) + group, BF16),
            pltpu.VMEM((depth, plane) + group, BF16),
            pltpu.VMEM((depth,) + block, BF16),
            pltpu.VMEM((depth,) + block, BF16),
            pltpu.VMEM((depth,) + block, BF16),
            pltpu.VMEM(block, F32),
            pltpu.VMEM((depth,) + block, BF16),
            pltpu.VMEM((depth, plane) + group, BF16),
            pltpu.VMEM((fronts,) + group, BF16),
            dma((plane,)),
            dma((plane,)),
            dma((depth, plane)),
            dma((depth, plane)),
            dma((depth,)),
            dma((depth,)),
            dma((depth,)),
            dma((depth,)),
            dma((depth,)),
            dma((depth,)),
            dma((depth, plane)),
            dma((depth, plane)),
            dma((depth,)),
            dma((rows,)),
            dma((depth, width)),
            dma((cols,)),
            dma((cols,)),
        ],
        cost_estimate=pl.CostEstimate(flops=10**10, bytes_accessed=10**7, transcendentals=0),
        compiler_params=pltpu.CompilerParams(vmem_limit_bytes=VMEM_LIMIT, collective_id=0, has_side_effects=True),
    )(bound_count, sep_owner, place, table, front_factor, rhs, coupling, sep_rhs, sep_factor, cell_weight, cell_pivot)
    gram = dot(row_tile.reshape(cols * cells, sources), col_tile.reshape(rows * cells, sources), NT) * (1.0 / sources)
    return (sep_potential, gram * gram)


def solution(mesh):
    both_axes = P(("row", "col"), None)
    placed = (both_axes, both_axes, both_axes, P(("row", "col"))) + (both_axes,) * 6
    return jax.shard_map(
        local,
        mesh=mesh,
        in_specs=placed,
        out_specs=(both_axes, P("row", "col")),
        check_vma=False,
    )
```

time: 186 us -> 112 us (0.60)
  waiting for transfers between devices: 72.8 us -> 0 us
  Pallas kernels: 46.3 us -> 101 us
  blocking collectives: 37.4 us -> 0 us
  starting transfers between devices: 17.7 us -> 0 us
    all_to_all x3 -> x0, waiting for transfers between devices: 72.8 us -> none  [the longest x1 41.6 us: local(): lax.all_to_all(replies.reshape(fronts, slots, sources), ('row', 'col'), s...]
    pallas_call x4 -> x1, Pallas kernels: 46.3 us -> 101 us  [local(): pl.pallas_call(functools.partial(whole_kernel, depth), out_shape=(shape(b...]
    all_gather x2 -> x0, blocking collectives: 37.4 us -> none  [the longest x1 31.5 us: local(): lax.all_gather(field, 'row', axis=0, tiled=True)]
    all_to_all x3 -> x0, starting transfers between devices: 17.7 us -> none  [the longest x1 7.33 us: local(): lax.all_to_all(out_index, ('row', 'col'), split_axis=0, concat_axis=0, ti...]
    reshape x2 -> x1, local copies, waits for them, and re-layouts: 2.76 us -> 0.09 us  [local(): sep_index.reshape(halves, 1, slots)]
    unnamed x6 -> x5, local copies, waits for them, and re-layouts: 1.44 us -> 3.63 us
  transfers between devices with their start and end apart: 3 -> 0, of which waited for: 2 -> 0; matrix products, arithmetic and copies ran while one was open for 3% -> 0% of each run, Pallas kernels for 15% -> 0%
where the time goes in v2:
time: 112 us
  Pallas kernels  101 us (90%)
  local copies, waits for them, and re-layouts  4.32 us (4%)
  matrix products  2.97 us (3%)
  other arithmetic  1.98 us (2%)
  between operations  1.3 us (1%)
    pallas_call x1, Pallas kernels, local(): pl.pallas_call(functools.partial(whole_kernel, depth), out_shape=(shape(b...  101 us
    unnamed x5, local copies, waits for them, and re-layouts  3.63 us
    dot_general x1, matrix products, dot(): return lax.dot_general(left, right, dims, preferred_element_type=F32)  2.97 us

profile of v2, /device:TPU:0, one launch (start us, length us, event | category | flops | bytes accessed | tf_op | source)
XLA Modules:
  0.0 111.6 jit_solution(7581543507370147275)
XLA Ops:
  1.3 1.3 %select_reduce_fusion.place_ref = s32[32]{0:T(128)} fusion(s32[16]{0:T(128)} %bitcast.7), kind=kLoop, calls=%fused_computation.1 | loop fusion | flops 1504 | bytes 192 | tf_op jit(solution)/shard_map/reduce_min | solution.py:436
  2.5 0.7 reduce
  3.3 0.1 reshape.13
  3.3 0.6 pad.4.table_ref
  4.0 1.4 %copy.14.weight_ref = f32[128,8]{1,0:T(8,128)} copy(f32[128,8]{0,1:T(8,128)} %param.18) | data formatting | bytes 8192 | tf_op args[8]
  5.4 1.4 %copy.15.pivot_ref = s32[128,8]{1,0:T(8,128)} copy(s32[128,8]{0,1:T(8,128)} %param.19) | data formatting | bytes 8192 | tf_op args[9]
  6.8 101.0 %shard_map.113 = (f32[512,256]{1,0:T(8,128)}, bf16[4,128,256]{2,1,0:T(8,128)(2,1)}, bf16[8,128,256]{2,1,0:T(8,128)(2,1)}) custom-call(s32[1]{0:T(128)S(6)} %copy.17.count_ref, s32[1,16]{1,0:T(1,128)} %owner_ref.1, s32[32]{0:T(128)} %select_reduce_fusion.place_ref, s32[17,1,112]{2,1,0:T(1,128)} %pad.4.table_ref, f32[1024,1024]{1,0:T(8,128)} %factor_ref.1, ...), custom_call_target="tpu_custom_call" | custom-call | flops 10000000000 | bytes 10000000 | tf_op jit(solution)/shard_map/pallas_call | solution.py:441
  107.8 0.0 copy-start
  107.8 3.0 %multiply_multiply_fusion = f32[512,1024]{1,0:T(8,128)} fusion(bf16[512,256]{1,0:T(8,128)(2,1)} %bitcast.6, bf16[1024,256]{1,0:T(8,128)(2,1)} %bitcast.5), kind=kOutput, calls=%fused_computation | convolution fusion | flops 269484032 | bytes 2883584 | tf_op jit(solution)/shard_map/dot_general | solution.py:23
  110.8 0.0 copy-done
  110.8 0.8 copy.18
Async XLA Ops:
  107.8 3.0 %copy-start = (f32[512,256]{1,0:T(8,128)S(1)}, f32[512,256]{1,0:T(8,128)}, u32[]{:S(2)}) copy-start(f32[512,256]{1,0:T(8,128)} %get-tuple-element.10) | copy-start | bytes 1572868

commit v3 on v2

--- a/solution.py
+++ b/solution.py
@@ -27,7 +27,7 @@
     return dot(left[0], right[0], dims) + (dot(left[0], right[1], dims) + dot(left[1], right[0], dims))
 
 
-def invert(factor_ref, high_ref, low_ref, work_ref):
+def invert(factor_ref, high_ref, low_ref, work_ref, ready):
     order = factor_ref.shape[0]
     base = work_ref.shape[1]
     count = order // base
@@ -42,6 +42,7 @@
         return factor_ref[pl.ds(block * base, base), pl.ds(block * base, base)]
 
     for block in range(count):
+        ready(block, block)
         part = diagonal(block)
         only = jnp.where(differ == 0, part, 0.0)
         down = 1.0 / jnp.sum(only, axis=1, keepdims=True)
@@ -67,6 +68,9 @@
     while size < order:
         for start in range(0, order, 2 * size):
             first, second = pl.ds(start, size), pl.ds(start + size, size)
+            for down in range(size // base):
+                for across in range(size // base):
+                    ready((start + size) // base + down, start // base + across)
             outer = split(factor_ref[second, first])
             step = split(dot3(outer, (high_ref[first, first], low_ref[first, first])))
             high, low = split(-dot3((high_ref[second, second], low_ref[second, second]), step))
@@ -90,11 +94,11 @@
     owner_ref,
     place_ref,
     table_ref,
-    factor_ref,
+    factor_hbm,
     rhs_ref,
-    coupling_ref,
+    coupling_hbm,
     sep_rhs_ref,
-    sep_factor_ref,
+    sep_factor_hbm,
     weight_ref,
     pivot_ref,
     sep_out_ref,
@@ -103,6 +107,9 @@
     high_ref,
     low_ref,
     work_ref,
+    factor_ref,
+    sep_factor_ref,
+    coupling_ref,
     sep_high_ref,
     sep_low_ref,
     sep_work_ref,
@@ -137,7 +144,33 @@
     next_send,
     row_send,
     row_recv,
+    spread_ref,
+    turned_rhs_ref,
+    factor_load,
+    sep_load,
+    coupling_load,
 ):
+    base = work_ref.shape[1]
+
+    def load(source, target, sems, down, across):
+        spot = (pl.ds(down * base, base), pl.ds(across * base, base))
+        return pltpu.make_async_copy(source.at[spot], target.at[spot], sems.at[down, across])
+
+    def front_block(down, across):
+        return load(factor_hbm, factor_ref, factor_load, down, across)
+
+    def sep_block(down, across):
+        return load(sep_factor_hbm, sep_factor_ref, sep_load, down, across)
+
+    def each_block(count, action):
+        for away in range(count):
+            for down in range(away, count):
+                action(down, down - away)
+
+    coupling_copy = pltpu.make_async_copy(coupling_hbm, coupling_ref, coupling_load)
+    each_block(work_ref.shape[0], lambda down, across: front_block(down, across).start())
+    coupling_copy.start()
+    each_block(sep_work_ref.shape[0], lambda down, across: sep_block(down, across).start())
     rows, cols = col_out_ref.shape[0], row_out_ref.shape[0]
     width = rows // depth
     plane = width * cols
@@ -228,7 +261,7 @@
     def near_first(at):
         return z + ((at + 1) // 2) * (1 - 2 * (at % 2))
 
-    invert(factor_ref, high_ref, low_ref, work_ref)
+    invert(factor_ref, high_ref, low_ref, work_ref, lambda down, across: front_block(down, across).wait())
     pl.semaphore_wait(barrier, plane + depth - 2)
 
     def fill_index(spot, carry):
@@ -242,6 +275,7 @@
 
     turned_rhs = rhs_ref[...].T
     solved = turned_solve(turned_rhs, high_ref, low_ref).astype(BF16)
+    coupling_copy.wait()
     product = dot(coupling_ref[...], solved, NT)
     live = lax.broadcasted_iota(jnp.int32, product.shape, 0) < count_ref[0]
     flat_ref[...] = jnp.where(live, product, 0.0).astype(BF16)
@@ -258,7 +292,7 @@
         received_ref[high, me] = contrib_ref[place_ref[high * plane + me]]
 
     levels(far_first, send_out)
-    invert(sep_factor_ref, sep_high_ref, sep_low_ref, sep_work_ref)
+    invert(sep_factor_ref, sep_high_ref, sep_low_ref, sep_work_ref, lambda down, across: sep_block(down, across).wait())
     others(lambda spot: index_arrival(spot).wait_recv())
     for high in range(depth):
         column_ref[high] = jnp.concatenate([index_ref[spot, high] for spot in range(plane)], axis=0).T
@@ -324,20 +358,24 @@
         returned_ref[high * plane + me] = reply_ref[high, me]
 
     levels(near_first, pass_on)
-    shape = (weight_ref.shape[0], rhs_ref.shape[0])
+    weight, pivot = weight_ref[...].T, pivot_ref[...].T
+    shape = (weight.shape[0], rhs_ref.shape[0])
     spots = lax.broadcasted_iota(jnp.int32, shape, 1)
     spread = jnp.zeros(shape, F32)
-    for near in range(weight_ref.shape[1]):
-        spread += jnp.where(spots == pivot_ref[:, near : near + 1], weight_ref[:, near : near + 1], 0.0)
+    for near in range(weight.shape[1]):
+        spread += jnp.where(spots == pivot[:, near : near + 1], weight[:, near : near + 1], 0.0)
+    spread_high, spread_low = split(spread)
+    spread_ref[0], spread_ref[1] = spread_high, spread_low
+    turned_rhs_ref[...] = rhs_ref[...].T
     levels(near_first, lambda high: others(lambda spot: reply_arrival(high, spot).wait_recv()))
     for half in range(halves):
         flat_ref[pl.ds(half * slots, slots), :] = returned_ref[owner_ref[0, half]]
     values = flat_ref[...]
     live = lax.broadcasted_iota(jnp.int32, values.shape, 0) < count_ref[0]
-    values = jnp.where(live, values.astype(F32), 0.0)
-    lifted = dot(values.T.astype(BF16), coupling_ref[...], NN)
-    potential = turned_solve(rhs_ref[...].T - lifted, high_ref, low_ref)
-    field = dot3(split(spread), split(potential), NT).astype(BF16)
+    values = jnp.where(live, values.astype(F32), 0.0).astype(BF16)
+    lifted = dot(values.T, coupling_ref[...], NN)
+    potential = turned_solve(turned_rhs_ref[...] - lifted, high_ref, low_ref)
+    field = dot3((spread_ref[0], spread_ref[1]), split(potential), NT).astype(BF16)
     col_out_ref[row] = field
     row_out_ref[col] = field
 
@@ -432,6 +470,7 @@
     shape = jax.ShapeDtypeStruct
     smem = pl.BlockSpec(memory_space=pltpu.SMEM)
     vmem = pl.BlockSpec(memory_space=pltpu.VMEM)
+    hbm = pl.BlockSpec(memory_space=pl.ANY)
     found = sep_owner[0][None, :] == jnp.arange(fronts, dtype=jnp.int32)[:, None]
     place = jnp.min(jnp.where(found, jnp.arange(halves, dtype=jnp.int32)[None, :], halves), axis=1)
     table = jnp.pad(sep_index.reshape(halves, 1, slots), ((0, 1), (0, 0), (0, 0)), constant_values=-1)
@@ -445,12 +484,15 @@
             shape((cols, cells, sources), BF16),
             shape((rows, cells, sources), BF16),
         ),
-        in_specs=[smem] * 3 + [vmem] * 8,
+        in_specs=[smem] * 3 + [vmem, hbm, vmem, hbm, vmem, hbm, vmem, vmem],
         out_specs=(vmem, vmem, vmem),
         scratch_shapes=[
             pltpu.VMEM((pivots, pivots), BF16),
             pltpu.VMEM((pivots, pivots), BF16),
             pltpu.VMEM((pivots // base, base, base), F32),
+            pltpu.VMEM((pivots, pivots), F32),
+            pltpu.VMEM((sep_size, sep_size), F32),
+            pltpu.VMEM((bound, pivots), BF16),
             pltpu.VMEM((sep_size, sep_size), BF16),
             pltpu.VMEM((sep_size, sep_size), BF16),
             pltpu.VMEM((sep_size // base, base, base), F32),
@@ -485,10 +527,15 @@
             dma((depth, width)),
             dma((cols,)),
             dma((cols,)),
+            pltpu.VMEM((2, cells, pivots), BF16),
+            pltpu.VMEM((sources, pivots), F32),
+            dma((pivots // base, pivots // base)),
+            dma((sep_size // base, sep_size // base)),
+            dma,
         ],
         cost_estimate=pl.CostEstimate(flops=10**10, bytes_accessed=10**7, transcendentals=0),
         compiler_params=pltpu.CompilerParams(vmem_limit_bytes=VMEM_LIMIT, collective_id=0, has_side_effects=True),
-    )(bound_count, sep_owner, place, table, front_factor, rhs, coupling, sep_rhs, sep_factor, cell_weight, cell_pivot)
+    )(bound_count, sep_owner, place, table, front_factor, rhs, coupling, sep_rhs, sep_factor, cell_weight.T, cell_pivot.T)
     gram = dot(row_tile.reshape(cols * cells, sources), col_tile.reshape(rows * cells, sources), NT) * (1.0 / sources)
     return (sep_potential, gram * gram)
 

time: 112 us -> 108 us (0.964)
  local copies, waits for them, and re-layouts: 4.32 us -> 1.49 us
    unnamed x5 -> x3, local copies, waits for them, and re-layouts: 3.63 us -> 0.8 us
where the time goes in v3:
time: 108 us
  Pallas kernels  100 us (93%)
  matrix products  2.97 us (3%)
  other arithmetic  1.97 us (2%)
  local copies, waits for them, and re-layouts  1.49 us (1%)
  between operations  1.3 us (1%)
    pallas_call x1, Pallas kernels, local(): pl.pallas_call(functools.partial(whole_kernel, depth), out_shape=(shape(b...  100 us
    dot_general x1, matrix products, dot(): return lax.dot_general(left, right, dims, preferred_element_type=F32)  2.97 us

profile of v3, /device:TPU:0, one launch (start us, length us, event | category | flops | bytes accessed | tf_op | source)
XLA Modules:
  0.0 107.9 jit_solution(12772651329978428370)
XLA Ops:
  1.3 1.3 %select_reduce_fusion.place_ref = s32[32]{0:T(128)} fusion(s32[16]{0:T(128)} %bitcast.11), kind=kLoop, calls=%fused_computation.1 | loop fusion | flops 1504 | bytes 192 | tf_op jit(solution)/shard_map/reduce_min | solution.py:475
  2.5 0.7 reduce
  3.2 0.1 reshape.13
  3.3 0.6 pad.4.table_ref
  3.9 100.2 %shard_map.113 = (f32[512,256]{1,0:T(8,128)}, bf16[4,128,256]{2,1,0:T(8,128)(2,1)}, bf16[8,128,256]{2,1,0:T(8,128)(2,1)}) custom-call(s32[1]{0:T(128)S(6)} %copy.13.count_ref, s32[1,16]{1,0:T(1,128)} %owner_ref.1, s32[32]{0:T(128)} %select_reduce_fusion.place_ref, s32[17,1,112]{2,1,0:T(1,128)} %pad.4.table_ref, f32[1024,1024]{1,0:T(8,128)} %factor_hbm.1, ...), custom_call_target="tpu_custom_call" | custom-call | flops 10000000000 | bytes 10000000 | tf_op jit(solution)/shard_map/pallas_call | solution.py:480
  104.2 0.0 copy-start
  104.2 3.0 %multiply_multiply_fusion = f32[512,1024]{1,0:T(8,128)} fusion(bf16[512,256]{1,0:T(8,128)(2,1)} %bitcast.8, bf16[1024,256]{1,0:T(8,128)(2,1)} %bitcast.7), kind=kOutput, calls=%fused_computation | convolution fusion | flops 269484032 | bytes 2883584 | tf_op jit(solution)/shard_map/dot_general | solution.py:23
  107.1 0.0 copy-done
  107.1 0.8 copy.14
Async XLA Ops:
  104.2 3.0 %copy-start = (f32[512,256]{1,0:T(8,128)S(1)}, f32[512,256]{1,0:T(8,128)}, u32[]{:S(2)}) copy-start(f32[512,256]{1,0:T(8,128)} %get-tuple-element.10) | copy-start | bytes 1572868

commit v4 on v3

--- a/solution.py
+++ b/solution.py
@@ -298,10 +298,14 @@
         column_ref[high] = jnp.concatenate([index_ref[spot, high] for spot in range(plane)], axis=0).T
 
     def gather_in(high):
-        others(lambda spot: out_arrival(high, spot).wait_recv())
         numbers = lax.broadcasted_iota(jnp.int32, (sep_size, slots), 0)
         own_ref[...] = jnp.zeros_like(own_ref)
         for spot in range(plane):
+
+            @pl.when(me != spot)
+            def _():
+                out_arrival(high, spot).wait_recv()
+
             selector = jnp.where(numbers == index_ref[spot, high], 1.0, 0.0).astype(BF16)
             own_ref[...] += dot(selector, received_ref[high, spot], NN)
 

time: 108 us -> 108 us (level); the launches traced: 108 us -> 107 us
    pallas_call x1, Pallas kernels: 100 us -> 99 us  [local(): pl.pallas_call(functools.partial(whole_kernel, depth), out_shape=(shape(b...]
where the time goes in v4:
time: 108 us; the launch traced here: 107 us
  Pallas kernels  99 us (92%)
  matrix products  2.97 us (3%)
  other arithmetic  1.97 us (2%)
  local copies, waits for them, and re-layouts  1.49 us (1%)
  between operations  1.3 us (1%)
    pallas_call x1, Pallas kernels, local(): pl.pallas_call(functools.partial(whole_kernel, depth), out_shape=(shape(b...  99 us
    dot_general x1, matrix products, dot(): return lax.dot_general(left, right, dims, preferred_element_type=F32)  2.97 us

profile of v4, /device:TPU:0, one launch (start us, length us, event | category | flops | bytes accessed | tf_op | source)
XLA Modules:
  0.0 106.7 jit_solution(5641091587985931399)
XLA Ops:
  1.3 1.3 %select_reduce_fusion.place_ref = s32[32]{0:T(128)} fusion(s32[16]{0:T(128)} %bitcast.11), kind=kLoop, calls=%fused_computation.1 | loop fusion | flops 1504 | bytes 192 | tf_op jit(solution)/shard_map/reduce_min | solution.py:479
  2.5 0.7 reduce
  3.2 0.1 reshape.13
  3.3 0.6 pad.4.table_ref
  3.9 99.0 %shard_map.113 = (f32[512,256]{1,0:T(8,128)}, bf16[4,128,256]{2,1,0:T(8,128)(2,1)}, bf16[8,128,256]{2,1,0:T(8,128)(2,1)}) custom-call(s32[1]{0:T(128)S(6)} %copy.13.count_ref, s32[1,16]{1,0:T(1,128)} %owner_ref.1, s32[32]{0:T(128)} %select_reduce_fusion.place_ref, s32[17,1,112]{2,1,0:T(1,128)} %pad.4.table_ref, f32[1024,1024]{1,0:T(8,128)} %factor_hbm.1, ...), custom_call_target="tpu_custom_call" | custom-call | flops 10000000000 | bytes 10000000 | tf_op jit(solution)/shard_map/pallas_call | solution.py:484
  103.0 0.0 copy-start
  103.0 3.0 %multiply_multiply_fusion = f32[512,1024]{1,0:T(8,128)} fusion(bf16[512,256]{1,0:T(8,128)(2,1)} %bitcast.8, bf16[1024,256]{1,0:T(8,128)(2,1)} %bitcast.7), kind=kOutput, calls=%fused_computation | convolution fusion | flops 269484032 | bytes 2883584 | tf_op jit(solution)/shard_map/dot_general | solution.py:23
  105.9 0.0 copy-done
  105.9 0.8 copy.14
Async XLA Ops:
  103.0 3.0 %copy-start = (f32[512,256]{1,0:T(8,128)S(1)}, f32[512,256]{1,0:T(8,128)}, u32[]{:S(2)}) copy-start(f32[512,256]{1,0:T(8,128)} %get-tuple-element.10) | copy-start | bytes 1572868
